TPU v7x, 128 devices: a whole 4x4x4 slice. The times are simulated.
128 devices in a mesh: tm: 32 (over z, y, x_hi), clip: 4 (over x_lo, core).
Axes of the slice: x: 4 (x_hi: 2, x_lo: 2; x = x_hi * 2 + x_lo), y: 4, z: 4, core: 2. Of those that a mesh axis runs over, the one named last changes fastest.
Arguments:
- student_query: bfloat16 [16384, 1024], P('tm', 'clip'), may hold values from -12 to 12
- teacher_key: bfloat16 [65536, 1024], P('tm', 'clip'), may hold values from -1000 to 1000
- teacher_value: bfloat16 [65536, 1024], P('tm', 'clip'), may hold values from -12 to 12
- clip_order: int32 [65536], replicated, may hold values from 0 to 65535, as said below
- band_start: int32 [512], P('tm'), may hold values from -16 to -1
- band_end: int32 [512], P('tm'), may hold values from 1 to 16
- output_weight: bfloat16 [1024, 1024], P('clip'), may hold values from -0.1875 to 0.1875
- cotangent: bfloat16 [16384, 1024], P('tm', 'clip'), may hold values from -6 to 6
Outputs:
- joined: bfloat16 [16384, 1024], P('tm', 'clip')
- grad_query: bfloat16 [16384, 1024], P('tm', 'clip')
- grad_output_weight: float32 [1024, 1024], P('clip')
Inputs may be any that keep to these rules, and one draw needn't show every extreme that they name: clip_order is a permutation. For a time row t of time shard j = t // 2048, clip_order[t] % 2048 lies in [j * 64, (j + 1) * 64): every input shard holds exactly 64 rows of every time shard, as one run.
All inputs are finite; a program needn't handle non-finite values.
Results may differ from a plain program's by a relative error of at most 0.0094.
Values may be sent and summed in bfloat16 or wider, within the bound.
A program may use at most 128 MiB of HBM per device.

v0:
```python
import math

import jax
import jax.numpy as jnp
from jax import lax
from jax.sharding import PartitionSpec as P

HDIM = 64
SBLK = 32
TBLK = 128


def with_halo(cells, sides, width):
    for axis, dim in sides:
        count = lax.axis_size(axis)
        ends = count - 1
        head = lax.slice_in_dim(cells, 0, width, axis=dim)
        tail = lax.slice_in_dim(cells, cells.shape[dim] - width, cells.shape[dim], axis=dim)
        cells = jnp.concatenate(
            [
                lax.ppermute(tail, axis, [(i, (i + 1) % count) for i in range(ends)]),
                cells,
                lax.ppermute(head, axis, [((i + 1) % count, i) for i in range(ends)]),
            ],
            axis=dim,
        )
    return cells


def on_device(
    student_query,
    teacher_key,
    teacher_value,
    clip_order,
    band_start,
    band_end,
    output_weight,
    cotangent,
):
    shards = lax.axis_size("tm")
    self_index = lax.axis_index("tm")
    student_rows = student_query.shape[0]
    teacher_rows = teacher_key.shape[0]
    features = student_query.shape[1]
    piece_rows = teacher_rows // shards
    stacked = jnp.stack((teacher_key, teacher_value))
    arrived = lax.all_to_all(stacked, "tm", split_axis=1, concat_axis=1, tiled=True)
    lookup = lax.dynamic_slice_in_dim(clip_order, self_index * teacher_rows, teacher_rows)
    ordered = jnp.take(arrived, lookup // teacher_rows * piece_rows + lookup % piece_rows, axis=1)
    padded = with_halo(ordered, (("tm", 1),), teacher_rows)
    keys_wide = padded[0]
    values_wide = padded[1]
    upstream_full = lax.all_gather(cotangent, "clip", axis=1, tiled=True)
    attn_grad = lax.dot_general(
        upstream_full, output_weight, (((1,), (1,)), ((), ())), preferred_element_type=jnp.float32
    ).astype(jnp.bfloat16)
    heads_here = features // HDIM
    head_group = min(2, heads_here)
    group_width = head_group * HDIM
    query_block = min(256, student_rows)
    block_count = student_rows // query_block
    group_count = heads_here // head_group
    window = 4 * query_block + 2 * teacher_rows
    scaling = 1.0 / math.sqrt(HDIM)
    blocks_here = student_rows // SBLK
    base_block = self_index * blocks_here
    total_blocks = shards * blocks_here

    def attend_item(item_index):
        head_slot = item_index // block_count
        query_slot = item_index % block_count
        row_start = query_slot * query_block
        col_start = head_slot * group_width
        query_part = lax.dynamic_slice(
            student_query, (row_start, col_start), (query_block, group_width)
        ).reshape(query_block, head_group, HDIM)
        grad_part = lax.dynamic_slice(
            attn_grad, (row_start, col_start), (query_block, group_width)
        ).reshape(query_block, head_group, HDIM)
        key_part = lax.dynamic_slice(
            keys_wide, (4 * row_start, col_start), (window, group_width)
        ).reshape(window, head_group, HDIM)
        value_part = lax.dynamic_slice(
            values_wide, (4 * row_start, col_start), (window, group_width)
        ).reshape(window, head_group, HDIM)
        scores = (
            jnp.einsum("qhd,khd->hqk", query_part, key_part, preferred_element_type=jnp.float32)
            * scaling
        )
        local_block = (row_start + jnp.arange(query_block, dtype=jnp.int32)) // SBLK
        global_block = base_block + local_block
        band_low = global_block + band_start[local_block]
        band_high = global_block + band_end[local_block]
        key_block = (self_index - 1) * blocks_here + (
            4 * row_start + jnp.arange(window, dtype=jnp.int32)
        ) // TBLK
        valid = (key_block[None, :] >= band_low[:, None]) & (
            key_block[None, :] <= band_high[:, None]
        )
        valid = valid & (key_block[None, :] >= 0) & (key_block[None, :] < total_blocks)
        scores = jnp.where(valid[None, :, :], scores, -jnp.inf)
        row_max = jnp.max(scores, axis=-1, keepdims=True)
        shifted = jnp.exp(scores - row_max)
        probs = shifted / jnp.sum(shifted, axis=-1, keepdims=True)
        weights = probs.astype(jnp.bfloat16)
        head_out = jnp.einsum(
            "hqk,khd->qhd", weights, value_part, preferred_element_type=jnp.float32
        ).astype(jnp.bfloat16)
        dprobs = jnp.einsum(
            "qhd,khd->hqk", grad_part, value_part, preferred_element_type=jnp.float32
        )
        delta = jnp.sum(probs * dprobs, axis=-1, keepdims=True)
        dscores = (probs * (dprobs - delta) * scaling).astype(jnp.bfloat16)
        query_grad = jnp.einsum(
            "hqk,khd->qhd", dscores, key_part, preferred_element_type=jnp.float32
        ).astype(jnp.bfloat16)
        return (
            head_out.reshape(query_block, group_width),
            query_grad.reshape(query_block, group_width),
        )

    outputs, gradients = lax.map(
        attend_item, jnp.arange(group_count * block_count, dtype=jnp.int32)
    )
    attention = (
        outputs.reshape(group_count, block_count, query_block, group_width)
        .transpose(1, 2, 0, 3)
        .reshape(student_rows, features)
    )
    grad_query = (
        gradients.reshape(group_count, block_count, query_block, group_width)
        .transpose(1, 2, 0, 3)
        .reshape(student_rows, features)
    )
    local_weight_grad = lax.dot_general(
        attention, upstream_full, (((0,), (0,)), ((), ())), preferred_element_type=jnp.float32
    )
    weight_grad = lax.psum(local_weight_grad, "tm")
    summed = lax.psum_scatter(
        jnp.dot(attention, output_weight, preferred_element_type=jnp.float32),
        "clip",
        scatter_dimension=1,
        tiled=True,
    )
    return (summed.astype(jnp.bfloat16), grad_query, weight_grad)


def solution(mesh):
    return jax.shard_map(
        on_device,
        mesh=mesh,
        in_specs=(
            P("tm", "clip"),
            P("tm", "clip"),
            P("tm", "clip"),
            P(),
            P("tm"),
            P("tm"),
            P("clip", None),
            P("tm", "clip"),
        ),
        out_specs=(P("tm", "clip"), P("tm", "clip"), P("clip", None)),
        check_vma=False,
    )
```

profile of v0, /device:TPU:0, one launch (start us, length us, event | category | flops | bytes accessed | tf_op | source)
XLA Modules:
  0.0 941.9 jit_solution(17299504331697858677)
XLA Ops:
  19.2 10.9 %all-to-all-start = ((bf16[2,2048,256]{2,0,1:T(2,128)(2,1)}), bf16[2,2048,256]{2,0,1:T(2,128)(2,1)S(1)}, u32[]{:S(2)}, u32[]{:S(2)}) async-start(bf16[2,2048,256]{2,0,1:T(2,128)(2,1)} %pad_maximum_fusion.1), calls=%async_computation | async-start | bytes 4194304 | tf_op jit(solution)/shard_map/all_to_all | solution.py:47
  30.9 29.8 %all-to-all-done = bf16[2,2048,256]{2,0,1:T(2,128)(2,1)S(1)} async-done(((bf16[2,2048,256]{2,0,1:T(2,128)(2,1)}), bf16[2,2048,256]{2,0,1:T(2,128)(2,1)S(1)}, u32[]{:S(2)}, u32[]{:S(2)}) %all-to-all-start) | async-done | bytes 2097184 | tf_op jit(solution)/shard_map/all_to_all | solution.py:47
  60.7 16.4 %gather_fusion = bf16[2048,2,256]{2,1,0:T(2,128)(2,1)} fusion(bf16[2,2048,256]{2,0,1:T(2,128)(2,1)S(1)} %all-to-all-done, s32[2048]{0:T(1024)S(1)} %broadcast_clamp_fusion), kind=kCustom, calls=%fused_computation | custom fusion | bytes 4202496 | tf_op jit(solution)/shard_map/jit(_take)/gather | solution.py:49
  77.1 9.2 fusion.21
  87.6 7.4 collective-permute-start
  95.1 27.0 %all-gather.2.cloned.1.call-done = bf16[512,1024]{1,0:T(8,128)(2,1)} async-done(((bf16[512,256]{1,0:T(8,128)(2,1)}), bf16[512,1024]{1,0:T(8,128)(2,1)}) %all-gather.2.cloned.1.call-update) | async-done | bytes 1048592 | tf_op jit(solution)/shard_map/all_gather | solution.py:53
  123.8 22.9 %collective-permute-done.1 = bf16[2,2048,256]{2,0,1:T(2,128)(2,1)} collective-permute-done((bf16[2,2048,256]{2,0,1:T(2,128)(2,1)S(1)}, bf16[2,2048,256]{2,0,1:T(2,128)(2,1)}, u32[]{:S(2)}, u32[]{:S(2)}) %collective-permute-start.1) | collective-permute-done | bytes 2097184 | tf_op jit(solution)/shard_map/ppermute | solution.py:23
  146.8 28.2 %pad_maximum_fusion = bf16[2,6144,256]{2,0,1:T(2,128)(2,1)S(1)} fusion(bf16[2,2048,256]{2,0,1:T(2,128)(2,1)} %collective-permute-done.1, bf16[2,2048,256]{2,0,1:T(2,128)(2,1)S(1)} %fusion.21, bf16[2,2048,256]{2,0,1:T(2,128)(2,1)} %collective-permute-done), kind=kLoop, calls=%fused_computation.67 | loop fusion | flops 6291456 | bytes 12582912 | tf_op jit(solution)/shard_map/concatenate | solution.py:19
  174.9 10.0 %fusion.36 = (bf16[1,6144,256]{2,0,1:T(2,128)(2,1)}, bf16[1,6144,256]{2,0,1:T(2,128)(2,1)}) fusion(bf16[2,6144,256]{2,0,1:T(2,128)(2,1)S(1)} %pad_maximum_fusion), kind=kLoop, calls=%fused_computation.97 | loop fusion | bytes 12582912 | tf_op jit(solution)/shard_map/slice | solution.py:51
  185.0 13.5 %copy.28 = bf16[1,6144,256]{1,2,0:T(8,128)(2,1)} copy(bf16[1,6144,256]{2,0,1:T(2,128)(2,1)} %get-tuple-element.319) | data formatting | bytes 6291456 | tf_op jit(solution)/shard_map/while | solution.py:122
  198.5 13.5 %copy.29 = bf16[1,6144,256]{1,2,0:T(8,128)(2,1)} copy(bf16[1,6144,256]{2,0,1:T(2,128)(2,1)} %get-tuple-element.318) | data formatting | bytes 6291456 | tf_op jit(solution)/shard_map/while | solution.py:122
  212.0 290.8 %while.15 = (s32[]{:T(128)}, bf16[4,256,128]{1,2,0:T(8,128)(2,1)}, bf16[4,256,128]{1,2,0:T(8,128)(2,1)}, s32[4]{0:T(128)S(1)}, bf16[6144,256]{0,1:T(8,128)(2,1)}...) while((s32[]{:T(128)}, bf16[4,256,128]{1,2,0:T(8,128)(2,1)}, ...), condition=%wide.region_4.5_spmd, body=%wide.region_0.4_spmd.sunk | while | flops 1383120128 | bytes 98125536 | solution.py:122
  222.6 8.9 compare_select_fusion.19
  244.2 6.0 fusion.79
  262.1 17.9 %multiply_convert_fusion.2 = bf16[2,256,5120]{2,1,0:T(8,128)(2,1)} fusion(f32[2,256,5120]{2,1,0:T(8,128)} %fusion.81, f32[2,256,5120]{2,1,0:T(8,128)} %get-tuple-element.483, f32[2,256]{1,0:T(2,128)S(1)} %get-tuple-element.484), kind=kOutput, calls=%fused_computation.3.clone.1 | output fusion | flops 18355712 | bytes 26216448 | tf_op jit(solution)/shard_map/while/body/eval_jaxpr/sub | solution.py:113
  295.3 8.9 compare_select_fusion.19
  316.9 6.0 fusion.79
  334.7 17.9 %multiply_convert_fusion.2 = bf16[2,256,5120]{2,1,0:T(8,128)(2,1)} fusion(f32[2,256,5120]{2,1,0:T(8,128)} %fusion.81, f32[2,256,5120]{2,1,0:T(8,128)} %get-tuple-element.483, f32[2,256]{1,0:T(2,128)S(1)} %get-tuple-element.484), kind=kOutput, calls=%fused_computation.3.clone.1 | output fusion | flops 18355712 | bytes 26216448 | tf_op jit(solution)/shard_map/while/body/eval_jaxpr/sub | solution.py:113
  367.9 8.9 compare_select_fusion.19
  407.4 17.9 %multiply_convert_fusion.2 = bf16[2,256,5120]{2,1,0:T(8,128)(2,1)} fusion(f32[2,256,5120]{2,1,0:T(8,128)} %fusion.81, f32[2,256,5120]{2,1,0:T(8,128)} %get-tuple-element.483, f32[2,256]{1,0:T(2,128)S(1)} %get-tuple-element.484), kind=kOutput, calls=%fused_computation.3.clone.1 | output fusion | flops 18355712 | bytes 26216448 | tf_op jit(solution)/shard_map/while/body/eval_jaxpr/sub | solution.py:113
  440.6 8.9 compare_select_fusion.19
  480.0 17.9 %multiply_convert_fusion.2 = bf16[2,256,5120]{2,1,0:T(8,128)(2,1)} fusion(f32[2,256,5120]{2,1,0:T(8,128)} %fusion.81, f32[2,256,5120]{2,1,0:T(8,128)} %get-tuple-element.483, f32[2,256]{1,0:T(2,128)S(1)} %get-tuple-element.484), kind=kOutput, calls=%fused_computation.3.clone.1 | output fusion | flops 18355712 | bytes 26216448 | tf_op jit(solution)/shard_map/while/body/eval_jaxpr/sub | solution.py:113
  508.2 65.7 %reduce-scatter.2.cloned.1.call-done = f32[512,256]{1,0:T(8,128)} async-done(((f32[512,1024]{1,0:T(8,128)}), f32[512,256]{1,0:T(8,128)}) %reduce-scatter.2.cloned.1.call-update) | async-done | bytes 524304 | tf_op jit(solution)/shard_map/reduce_scatter | solution.py:139
  575.7 357.4 %all-reduce.2.cloned.1.call-done = f32[256,1024]{1,0:T(8,128)} async-done(((f32[256,1024]{1,0:T(8,128)}), f32[256,1024]{1,0:T(8,128)}) %all-reduce.2.cloned.1.call-update) | async-done | bytes 1048592 | tf_op jit(solution)/shard_map/psum | solution.py:138
  (136 shorter events, 185.3 us)
Async XLA Ops:
  7.2 114.9 %copy-start = (bf16[256,1024]{1,0:T(8,128)(2,1)S(1)}, bf16[256,1024]{1,0:T(8,128)(2,1)}, u32[]{:S(2)}) copy-start(bf16[256,1024]{1,0:T(8,128)(2,1)} %param.16) | copy-start | bytes 1572868
  19.2 41.5 %all-to-all-start = ((bf16[2,2048,256]{2,0,1:T(2,128)(2,1)}), bf16[2,2048,256]{2,0,1:T(2,128)(2,1)S(1)}, u32[]{:S(2)}, u32[]{:S(2)}) async-start(bf16[2,2048,256]{2,0,1:T(2,128)(2,1)} %pad_maximum_fusion.1), calls=%async_computation | async-start | bytes 4194304 | tf_op jit(solution)/shard_map/all_to_all | solution.py:47
  30.2 92.0 %all-gather.2.cloned.1.call-start = ((), (), s32[]{:S(2)}) async-start(), calls=%async_computation.2 | async-start | bytes 1310720 | tf_op jit(solution)/shard_map/all_gather | solution.py:53
  86.3 60.4 %collective-permute-start.1 = (bf16[2,2048,256]{2,0,1:T(2,128)(2,1)S(1)}, bf16[2,2048,256]{2,0,1:T(2,128)(2,1)}, u32[]{:S(2)}, u32[]{:S(2)}) collective-permute-start(bf16[2,2048,256]{2,0,1:T(2,128)(2,1)S(1)} %fusion.21), channel_id=1, source_target_pairs={{4,0},{8,4},{12,8},{16,12},{20,16},{24,20},{28,24},{32,28},{36,32}... | collective-permute-start | bytes 6291464 | tf_op jit(solution)/shard_map/ppermute | solution.py:23
  87.6 59.1 %collective-permute-start = (bf16[2,2048,256]{2,0,1:T(2,128)(2,1)S(1)}, bf16[2,2048,256]{2,0,1:T(2,128)(2,1)}, u32[]{:S(2)}, u32[]{:S(2)}) collective-permute-start(bf16[2,2048,256]{2,0,1:T(2,128)(2,1)S(1)} %fusion.21), channel_id=1, source_target_pairs={{0,4},{4,8},{8,12},{12,16},{16,20},{20,24},{24,28},{28,32},{32,36}... | collective-permute-start | bytes 6291464 | tf_op jit(solution)/shard_map/ppermute | solution.py:21
  95.0 478.9 %reduce-scatter.2.cloned.1.call-start = ((), (), s32[]{:S(2)}) async-start(), calls=%async_computation.3 | async-start | bytes 2621440 | tf_op jit(solution)/shard_map/reduce_scatter | solution.py:139
  198.5 13.5 %copy-start.1 = (s32[16]{0:T(128)S(1)}, s32[16]{0:T(128)}, u32[]{:S(2)}) copy-start(s32[16]{0:T(128)} %param.14) | copy-start | bytes 196
  198.5 13.5 %copy-start.2 = (s32[16]{0:T(128)S(1)}, s32[16]{0:T(128)}, u32[]{:S(2)}) copy-start(s32[16]{0:T(128)} %param.15) | copy-start | bytes 196
  502.8 3.1 copy-start.3
  504.0 3.4 copy-start.4
  505.8 427.3 %all-reduce.2.cloned.1.call-start = ((), (), s32[]{:S(2)}) async-start(), calls=%async_computation.4 | async-start | bytes 2097152 | tf_op jit(solution)/shard_map/psum | solution.py:138
Sparse Core Ops, SparseCore 0:
  95.1 26.9 all-gather.1
  505.9 67.9 reduce-scatter.1
  577.0 356.0 all-reduce.1
where the time goes:
time: 945 us; the launch traced here: 942 us
  waiting for transfers between devices  503 us (53%)
  other arithmetic  228 us (24%)
  local copies, waits for them, and re-layouts  93.4 us (10%)
  matrix products  72.4 us (8%)
  starting transfers between devices  19.7 us (2%)
  between operations  13.9 us (1%)
  loops' own time  11.7 us (1%)
    psum x1, waiting for transfers between devices, on_device(): weight_grad = lax.psum(local_weight_grad, 'tm')  357 us
    sub x4, other arithmetic, attend_item(): dscores = (probs * (dprobs - delta) * scaling).astype(jnp.bfloat16)  71.7 us
    reduce_scatter x1, waiting for transfers between devices, on_device(): lax.psum_scatter(jnp.dot(attention, output_weight, preferred_element_type...  65.7 us
    gather x24, other arithmetic, attend_item(): band_low = global_block + band_start[local_block]  36.2 us
    all_to_all x1, waiting for transfers between devices, on_device(): lax.all_to_all(stacked, 'tm', split_axis=1, concat_axis=1, tiled=True)  29.8 us
    concatenate x1, other arithmetic, with_halo(): jnp.concatenate([lax.ppermute(tail, axis, [(i, (i + 1) % count) for i in...  28.2 us
    while x2, local copies, waits for them, and re-layouts, on_device(): lax.map(attend_item, jnp.arange(group_count * block_count, dtype=jnp.int32))  27 us
    all_gather x1, waiting for transfers between devices, on_device(): upstream_full = lax.all_gather(cotangent, 'clip', axis=1, tiled=True)  27 us
  transfers between devices with their start and end apart: 6, of which 5 were waited for; matrix products, arithmetic and copies ran while one was open for 1% of the time, Pallas kernels for 0%

commit v1 on v0

v1 whole, which is shorter than its diff:
```python
import functools
import math

import jax
import jax.numpy as jnp
from jax import lax
from jax.experimental import pallas as pl
from jax.experimental.pallas import tpu as pltpu
from jax.sharding import PartitionSpec as P

HDIM = 64
SBLK = 32
TBLK = 128
F = 128
CH = 256
ANY = pl.BlockSpec(memory_space=pl.ANY)
MESH = pl.DeviceIdType.MESH


def greet(shards, groups):
    me = lax.axis_index("tm")
    c = lax.axis_index("clip")
    barrier = pltpu.get_barrier_semaphore()

    def tell(d, carry):
        pl.semaphore_signal(
            barrier, inc=1, device_id={"tm": lax.rem(me + d, shards)}, device_id_type=MESH
        )
        return carry

    lax.fori_loop(1, shards, tell, 0)
    for d in range(1, groups):
        pl.semaphore_signal(
            barrier, inc=1, device_id={"clip": lax.rem(c + d, groups)}, device_id_type=MESH
        )
    pl.semaphore_wait(barrier, shards + groups - 2)


def scatter_kernel(
    shards, groups, tk, tv, sq, cot, ow, kv, cotf, wcols, qp,
    ks, kr, vs, vr, cs, cr, ws, wr, qs, qr, ls,
):
    me = lax.axis_index("tm")
    c = lax.axis_index("clip")
    half = lax.rem(me, 2)
    mate = me + 1 - 2 * half
    wide = cot.shape[1]
    greet(shards, groups)

    def key_copy(target, slot, src):
        p = lax.div(target, 2)
        col = pl.multiple_of(lax.rem(target, 2) * 128, 128)
        return (
            pltpu.make_async_remote_copy(
                src_ref=tk.at[pl.ds(2 * p, 2), :, pl.ds(col, 128)],
                dst_ref=kv.at[:, me, :, pl.ds(0, 128)],
                send_sem=ks.at[slot],
                recv_sem=kr.at[src],
                device_id={"tm": target},
                device_id_type=MESH,
            ),
            pltpu.make_async_remote_copy(
                src_ref=tv.at[pl.ds(2 * p, 2), :, pl.ds(col, 128)],
                dst_ref=kv.at[:, me, :, pl.ds(128, 128)],
                send_sem=vs.at[slot],
                recv_sem=vr.at[src],
                device_id={"tm": target},
                device_id_type=MESH,
            ),
        )

    def clip_copy(d, src):
        target = lax.rem(c + d, groups)
        mine = pl.multiple_of(c * wide, 128)
        theirs = pl.multiple_of(target * wide, 128)
        return (
            pltpu.make_async_remote_copy(
                src_ref=cot,
                dst_ref=cotf.at[:, pl.ds(mine, wide)],
                send_sem=cs.at[d],
                recv_sem=cr.at[src],
                device_id={"clip": target},
                device_id_type=MESH,
            ),
            pltpu.make_async_remote_copy(
                src_ref=ow.at[:, pl.ds(theirs, wide)],
                dst_ref=wcols.at[c],
                send_sem=ws.at[d],
                recv_sem=wr.at[src],
                device_id={"clip": target},
                device_id_type=MESH,
            ),
        )

    other = pl.multiple_of((1 - half) * 128, 128)
    own = pl.multiple_of(half * 128, 128)
    q_copy = pltpu.make_async_remote_copy(
        src_ref=sq.at[:, pl.ds(other, 128)],
        dst_ref=qp.at[half],
        send_sem=qs,
        recv_sem=qr,
        device_id={"tm": mate},
        device_id_type=MESH,
    )

    def start(d, carry):
        for copy in key_copy(lax.rem(me + d, shards), d, me):
            copy.start()
        return carry

    lax.fori_loop(1, shards, start, 0)
    for d in range(1, groups):
        for copy in clip_copy(d, c):
            copy.start()
    q_copy.start()
    mine = pl.multiple_of(c * wide, 128)
    pair = lax.div(me, 2)
    local = (
        pltpu.make_async_copy(
            tk.at[pl.ds(2 * pair, 2), :, pl.ds(own, 128)], kv.at[:, me, :, pl.ds(0, 128)], ls.at[0]
        ),
        pltpu.make_async_copy(
            tv.at[pl.ds(2 * pair, 2), :, pl.ds(own, 128)], kv.at[:, me, :, pl.ds(128, 128)], ls.at[1]
        ),
        pltpu.make_async_copy(cot, cotf.at[:, pl.ds(mine, wide)], ls.at[2]),
        pltpu.make_async_copy(ow.at[:, pl.ds(mine, wide)], wcols.at[c], ls.at[3]),
        pltpu.make_async_copy(sq.at[:, pl.ds(own, 128)], qp.at[half], ls.at[4]),
    )
    for copy in local:
        copy.start()

    def finish(d, carry):
        for copy in key_copy(lax.rem(me + d, shards), d, lax.rem(me + d, shards)):
            copy.wait()
        return carry

    for copy in local:
        copy.wait()
    q_copy.wait()
    for d in range(1, groups):
        for copy in clip_copy(d, lax.rem(c + d, groups)):
            copy.wait()
    lax.fori_loop(1, shards, finish, 0)


def scatter(tk, tv, sq, cot, ow, shards, groups):
    bf = jnp.bfloat16
    rows, wide = sq.shape
    dma = pltpu.SemaphoreType.DMA
    return pl.pallas_call(
        functools.partial(scatter_kernel, shards, groups),
        out_shape=(
            jax.ShapeDtypeStruct((2, shards, 64, 256), bf),
            jax.ShapeDtypeStruct((rows, groups * wide), bf),
            jax.ShapeDtypeStruct((groups, wide, wide), bf),
            jax.ShapeDtypeStruct((2, rows, 128), bf),
        ),
        in_specs=[ANY] * 5,
        out_specs=(ANY,) * 4,
        scratch_shapes=[
            dma((shards,)), dma((shards,)), dma((shards,)), dma((shards,)),
            dma((groups,)), dma((groups,)), dma((groups,)), dma((groups,)),
            dma(()), dma(()), dma((5,)),
        ],
        compiler_params=pltpu.CompilerParams(collective_id=0, has_side_effects=True),
        name="scatter",
    )(tk, tv, sq, cot, ow)


def sort_kernel(idx_ref, kv_ref, out_ref):
    i = pl.program_id(0)
    depth = kv_ref.shape[0]
    lane = lax.broadcasted_iota(jnp.int32, (128, 128), 1)
    for r in range(2):
        row = idx_ref[pl.ds(2 * i + r, 1), :]
        col = jnp.broadcast_to(row, (128, 128)).T
        hot = jnp.concatenate(
            [
                jnp.where(col == lane + 128 * k, 1.0, 0.0).astype(jnp.bfloat16)
                for k in range(depth // 128)
            ],
            axis=1,
        )
        out_ref[r * 128 : (r + 1) * 128, :] = jnp.dot(
            hot, kv_ref[...], preferred_element_type=jnp.float32
        ).astype(jnp.bfloat16)


def sort_rows(idx, kv):
    total = kv.shape[0]
    half = total // 2
    steps = total // 256
    per = half // 256
    return pl.pallas_call(
        sort_kernel,
        grid=(steps,),
        out_shape=jax.ShapeDtypeStruct((total, 256), jnp.bfloat16),
        in_specs=[
            pl.BlockSpec((total // 128, 128), lambda i: (0, 0)),
            pl.BlockSpec((half, 256), lambda i: (i // per, 0)),
        ],
        out_specs=pl.BlockSpec((256, 256), lambda i: (i, 0)),
        cost_estimate=pl.CostEstimate(
            flops=2 * total * half * 256, bytes_accessed=4 * total * 256, transcendentals=0
        ),
        name="sort_rows",
    )(idx, kv)


def attend_kernel(
    lo_ref, hi_ref, left, own, right, q_ref, g_ref, out_ref,
    kv, s_scr, d_scr, qb, gb, m_scr, l_scr, dd_scr, o_scr, sem,
):
    i = pl.program_id(0)
    side = left.shape[0]
    mid = own.shape[0]

    @pl.when(i == 0)
    def _():
        copies = (
            pltpu.make_async_copy(left, kv.at[pl.ds(0, side)], sem.at[0]),
            pltpu.make_async_copy(own, kv.at[pl.ds(side, mid)], sem.at[1]),
            pltpu.make_async_copy(right, kv.at[pl.ds(side + mid, side)], sem.at[2]),
        )
        for copy in copies:
            copy.start()
        for copy in copies:
            copy.wait()

    nb = F // SBLK
    los = [lo_ref[nb * i + r] for r in range(nb)]
    his = [hi_ref[nb * i + r] for r in range(nb)]
    low = functools.reduce(jnp.minimum, los)
    high = functools.reduce(jnp.maximum, his)
    per = CH // TBLK
    first = low // per
    count = high // per - first + 1

    lane = lax.broadcasted_iota(jnp.int32, (F, 128), 1)
    zero = jnp.zeros((F, 128), jnp.bfloat16)
    q = q_ref[...] * jnp.bfloat16(0.125)
    g = g_ref[...]
    qb[0:F, :] = jnp.where(lane < HDIM, q, zero)
    qb[F : 2 * F, :] = jnp.where(lane < HDIM, zero, q)
    gb[0:F, :] = jnp.where(lane < HDIM, g, zero)
    gb[F : 2 * F, :] = jnp.where(lane < HDIM, zero, g)
    m_scr[...] = jnp.full_like(m_scr, -jnp.inf)
    l_scr[...] = jnp.zeros_like(l_scr)
    dd_scr[...] = jnp.zeros_like(dd_scr)
    o_scr[...] = jnp.zeros_like(o_scr)
    nt = (((1,), (1,)), ((), ()))

    def first_pass(k, carry):
        base = pl.multiple_of((first + k) * CH, CH)
        keys = kv[pl.ds(base, CH), 0:128]
        values = kv[pl.ds(base, CH), 128:256]
        scores = lax.dot_general(qb[...], keys, nt, preferred_element_type=jnp.float32)
        for r in range(nb):
            for c in range(per):
                block = (first + k) * per + c
                ok = (block >= los[r]) & (block <= his[r])
                bias = jnp.where(ok, 0.0, -jnp.inf).astype(jnp.float32)
                for h in range(2):
                    a = h * F + r * SBLK
                    part = scores[a : a + SBLK, c * 128 : (c + 1) * 128] + bias
                    s_scr[k, a : a + SBLK, c * 128 : (c + 1) * 128] = part
                    m_scr[a : a + SBLK, :] = jnp.maximum(m_scr[a : a + SBLK, :], part)
        d_scr[k] = lax.dot_general(gb[...], values, nt, preferred_element_type=jnp.float32)
        return carry

    lax.fori_loop(0, count, first_pass, 0)
    m_scr[...] = jnp.broadcast_to(jnp.max(m_scr[...], axis=1, keepdims=True), m_scr.shape)

    def second_pass(k, carry):
        base = pl.multiple_of((first + k) * CH, CH)
        values = kv[pl.ds(base, CH), 128:256]
        top = m_scr[...]
        parts = []
        for c in range(per):
            part = jnp.exp(s_scr[k, :, c * 128 : (c + 1) * 128] - top)
            s_scr[k, :, c * 128 : (c + 1) * 128] = part
            l_scr[...] += part
            dd_scr[...] += part * d_scr[k, :, c * 128 : (c + 1) * 128]
            parts.append(part.astype(jnp.bfloat16))
        weights = jnp.concatenate(parts, axis=1)
        o_scr[...] += jnp.dot(weights, values, preferred_element_type=jnp.float32)
        return carry

    lax.fori_loop(0, count, second_pass, 0)
    inv = 1.0 / jnp.sum(l_scr[...], axis=1, keepdims=True)
    delta = jnp.sum(dd_scr[...], axis=1, keepdims=True) * inv
    m_scr[...] = jnp.broadcast_to(delta, m_scr.shape)
    l_scr[...] = jnp.broadcast_to(inv, l_scr.shape)
    out = o_scr[...] * l_scr[...]
    out_ref[:, 0:128] = jnp.where(lane < HDIM, out[0:F], out[F : 2 * F]).astype(jnp.bfloat16)
    o_scr[...] = jnp.zeros_like(o_scr)

    def third_pass(k, carry):
        base = pl.multiple_of((first + k) * CH, CH)
        keys = kv[pl.ds(base, CH), 0:128]
        centre = m_scr[...]
        parts = []
        for c in range(per):
            part = s_scr[k, :, c * 128 : (c + 1) * 128] * (
                d_scr[k, :, c * 128 : (c + 1) * 128] - centre
            )
            parts.append(part.astype(jnp.bfloat16))
        o_scr[...] += jnp.dot(
            jnp.concatenate(parts, axis=1), keys, preferred_element_type=jnp.float32
        )
        return carry

    lax.fori_loop(0, count, third_pass, 0)
    out = o_scr[...] * (l_scr[...] * 0.125)
    out_ref[:, 128:256] = jnp.where(lane < HDIM, out[0:F], out[F : 2 * F]).astype(jnp.bfloat16)


def attend(lo, hi, left, own, right, q, g):
    frames = q.shape[0]
    window = 2 * left.shape[0] + own.shape[0]
    reach = left.shape[0] // TBLK
    chunks = (2 * reach + F // SBLK) * TBLK // CH + 2
    f32 = jnp.float32
    return pl.pallas_call(
        attend_kernel,
        grid_spec=pltpu.PrefetchScalarGridSpec(
            num_scalar_prefetch=2,
            grid=(frames // F,),
            in_specs=[
                ANY, ANY, ANY,
                pl.BlockSpec((F, 128), lambda i, lo, hi: (i, 0)),
                pl.BlockSpec((F, 128), lambda i, lo, hi: (i, 0)),
            ],
            out_specs=pl.BlockSpec((F, 256), lambda i, lo, hi: (i, 0)),
            scratch_shapes=[
                pltpu.VMEM((window, 256), jnp.bfloat16),
                pltpu.VMEM((chunks, 2 * F, CH), f32),
                pltpu.VMEM((chunks, 2 * F, CH), f32),
                pltpu.VMEM((2 * F, 128), jnp.bfloat16),
                pltpu.VMEM((2 * F, 128), jnp.bfloat16),
                pltpu.VMEM((2 * F, 128), f32),
                pltpu.VMEM((2 * F, 128), f32),
                pltpu.VMEM((2 * F, 128), f32),
                pltpu.VMEM((2 * F, 128), f32),
                pltpu.SemaphoreType.DMA((3,)),
            ],
        ),
        out_shape=jax.ShapeDtypeStruct((frames, 256), jnp.bfloat16),
        cost_estimate=pl.CostEstimate(
            flops=8 * frames * 4096 * 256, bytes_accessed=6 << 20, transcendentals=frames * 8192
        ),
        name="attend",
    )(lo, hi, left, own, right, q, g)


def reduce_kernel(
    shards, groups, wg, o_ref, wsum, og, got, red, ss, sr, gs, gr, os_, or_, ls,
):
    me = lax.axis_index("tm")
    c = lax.axis_index("clip")
    wide = o_ref.shape[1]
    greet(shards, groups)

    def part_copy(target, slot, src):
        return pltpu.make_async_remote_copy(
            src_ref=wg.at[target],
            dst_ref=got.at[me],
            send_sem=ss.at[slot],
            recv_sem=sr.at[src],
            device_id={"tm": target},
            device_id_type=MESH,
        )

    def sum_copy(target, slot, src):
        return pltpu.make_async_remote_copy(
            src_ref=red,
            dst_ref=wsum.at[me],
            send_sem=gs.at[slot],
            recv_sem=gr.at[src],
            device_id={"tm": target},
            device_id_type=MESH,
        )

    def o_copy(d, src):
        mine = pl.multiple_of(c * wide, 128)
        return pltpu.make_async_remote_copy(
            src_ref=o_ref,
            dst_ref=og.at[:, pl.ds(mine, wide)],
            send_sem=os_.at[d],
            recv_sem=or_.at[src],
            device_id={"clip": lax.rem(c + d, groups)},
            device_id_type=MESH,
        )

    def start(d, carry):
        part_copy(lax.rem(me + d, shards), d, me).start()
        return carry

    def finish(d, carry):
        part_copy(lax.rem(me + d, shards), d, lax.rem(me + d, shards)).wait()
        return carry

    def start_sum(d, carry):
        sum_copy(lax.rem(me + d, shards), d, me).start()
        return carry

    def finish_sum(d, carry):
        sum_copy(lax.rem(me + d, shards), d, lax.rem(me + d, shards)).wait()
        return carry

    own = pltpu.make_async_copy(wg.at[me], got.at[me], ls.at[0])
    own.start()
    lax.fori_loop(1, shards, start, 0)
    for d in range(1, groups):
        o_copy(d, c).start()
    mine = pl.multiple_of(c * wide, 128)
    own_o = pltpu.make_async_copy(o_ref, og.at[:, pl.ds(mine, wide)], ls.at[1])
    own_o.start()
    own.wait()
    lax.fori_loop(1, shards, finish, 0)

    def add(s, acc):
        return acc + got[s].astype(jnp.float32)

    red[...] = lax.fori_loop(
        0, shards, add, jnp.zeros(red.shape, jnp.float32)
    ).astype(jnp.bfloat16)
    lax.fori_loop(1, shards, start_sum, 0)
    own_sum = pltpu.make_async_copy(red, wsum.at[me], ls.at[2])
    own_sum.start()
    own_o.wait()
    for d in range(1, groups):
        o_copy(d, lax.rem(c + d, groups)).wait()
    own_sum.wait()
    lax.fori_loop(1, shards, finish_sum, 0)


def reduce_all(wg, o, shards, groups):
    bf = jnp.bfloat16
    dma = pltpu.SemaphoreType.DMA
    _, part, cols = wg.shape
    rows, wide = o.shape
    return pl.pallas_call(
        functools.partial(reduce_kernel, shards, groups),
        out_shape=(
            jax.ShapeDtypeStruct((shards, part, cols), bf),
            jax.ShapeDtypeStruct((rows, groups * wide), bf),
        ),
        in_specs=[ANY] * 2,
        out_specs=(ANY,) * 2,
        scratch_shapes=[
            pltpu.VMEM((shards, part, cols), bf),
            pltpu.VMEM((part, cols), bf),
            dma((shards,)), dma((shards,)), dma((shards,)), dma((shards,)),
            dma((groups,)), dma((groups,)), dma((3,)),
        ],
        compiler_params=pltpu.CompilerParams(collective_id=1, has_side_effects=True),
        name="reduce_all",
    )(wg, o)


def on_device(
    student_query,
    teacher_key,
    teacher_value,
    clip_order,
    band_start,
    band_end,
    output_weight,
    cotangent,
):
    shards = lax.axis_size("tm")
    groups = lax.axis_size("clip")
    me = lax.axis_index("tm")
    half = me % 2
    pair = me // 2
    rows, wide = student_query.shape
    trows = teacher_key.shape[0]
    piece = trows // shards
    blocks = rows // SBLK
    f32 = jnp.float32
    bf = jnp.bfloat16

    kv, cot_full, w_cols, q_pair = scatter(
        teacher_key.reshape(shards, piece, wide),
        teacher_value.reshape(shards, piece, wide),
        student_query, cotangent, output_weight, shards, groups,
    )

    lookup = lax.dynamic_slice_in_dim(clip_order, pair * 2 * trows, 2 * trows)
    idx = lookup // trows * piece + lookup % piece
    own = sort_rows(idx.reshape(2 * trows // 128, 128), kv.reshape(2 * trows, 256))

    up = [(i, i + 2) for i in range(shards - 2)]
    down = [(i + 2, i) for i in range(shards - 2)]
    swap = [(i, i ^ 1) for i in range(shards)]
    left = lax.ppermute(own[trows:], "tm", up)
    right = lax.ppermute(own[:trows], "tm", down)

    grad = lax.dot_general(
        cot_full, output_weight, (((1,), (1,)), ((), ())), preferred_element_type=f32
    ).astype(bf)
    grad_own = lax.dynamic_slice_in_dim(grad, half * 128, 128, axis=1)
    grad_mate = lax.ppermute(
        lax.dynamic_slice_in_dim(grad, (1 - half) * 128, 128, axis=1), "tm", swap
    )
    first = half == 0
    g_pair = jnp.concatenate(
        [jnp.where(first, grad_own, grad_mate), jnp.where(first, grad_mate, grad_own)], axis=0
    )

    bands = jnp.stack([band_start, band_end])
    bands_mate = lax.ppermute(bands, "tm", swap)
    bands = jnp.concatenate(
        [jnp.where(first, bands, bands_mate), jnp.where(first, bands_mate, bands)], axis=1
    )
    reach = trows // TBLK
    base = pair * 2 * blocks
    at = reach + jnp.arange(2 * blocks, dtype=jnp.int32)
    total = shards * blocks
    lo = jnp.maximum(at + bands[0], reach - base)
    hi = jnp.minimum(at + bands[1], total - 1 + reach - base)

    od = attend(lo, hi, left, own, right, q_pair.reshape(2 * rows, 128), g_pair)

    mine = lax.dynamic_slice_in_dim(od, half * rows, rows, axis=0)
    back = lax.ppermute(
        lax.dynamic_slice_in_dim(od, (1 - half) * rows, rows, axis=0), "tm", swap
    )
    lower = jnp.where(first, mine, back)
    upper = jnp.where(first, back, mine)
    attention = jnp.concatenate([lower[:, :128], upper[:, :128]], axis=1)
    grad_query = jnp.concatenate([lower[:, 128:], upper[:, 128:]], axis=1)

    local = lax.dot_general(
        attention, cot_full, (((0,), (0,)), ((), ())), preferred_element_type=f32
    ).astype(bf)
    wsum, o_full = reduce_all(
        local.reshape(shards, wide // shards, groups * wide), attention, shards, groups
    )
    joined = jnp.dot(
        o_full, w_cols.reshape(groups * wide, wide), preferred_element_type=f32
    ).astype(bf)
    weight_grad = wsum.reshape(wide, groups * wide).astype(f32)
    return (joined, grad_query, weight_grad)


def solution(mesh):
    return jax.shard_map(
        on_device,
        mesh=mesh,
        in_specs=(
            P("tm", "clip"),
            P("tm", "clip"),
            P("tm", "clip"),
            P(),
            P("tm"),
            P("tm"),
            P("clip", None),
            P("tm", "clip"),
        ),
        out_specs=(P("tm", "clip"), P("tm", "clip"), P("clip", None)),
        check_vma=False,
    )
```

time: 945 us -> 217 us (0.23)
  waiting for transfers between devices: 503 us -> 26 us
  other arithmetic: 228 us -> 8.96 us
  Pallas kernels: 0 us -> 165 us
  local copies, waits for them, and re-layouts: 93.4 us -> 2.9 us
  matrix products: 72.4 us -> 4.12 us
  between operations: 13.9 us -> 0.77 us
  loops' own time: 11.7 us -> 0 us
    psum x1 -> x0, waiting for transfers between devices: 357 us -> none  [on_device(): weight_grad = lax.psum(local_weight_grad, 'tm')]
    pallas_call x0 -> x4, Pallas kernels: none -> 165 us  [the longest x1 54 us: scatter(): pl.pallas_call(functools.partial(scatter_kernel, shards, groups), out_sha...]
    sub x8 -> x0, other arithmetic: 95.5 us -> none  [the longest x4 71.7 us: attend_item(): dscores = (probs * (dprobs - delta) * scaling).astype(jnp.bfloat16)]
    dot_general x19 -> x3, matrix products: 72.4 us -> 4.12 us  [the longest x1 2.37 us: on_device(): jnp.dot(o_full, w_cols.reshape(groups * wide, wide), preferred_element_ty...]
    reduce_scatter x1 -> x0, waiting for transfers between devices: 65.7 us -> none  [on_device(): lax.psum_scatter(jnp.dot(attention, output_weight, preferred_element_type...]
    add x12 -> x0, other arithmetic: 44.7 us -> none  [the longest x4 22.4 us: attend_item(): band_high = global_block + band_end[local_block]]
    gather x25 -> x0, other arithmetic: 36.2 us -> none  [the longest x24 36.2 us: attend_item(): band_low = global_block + band_start[local_block]]
    all_to_all x1 -> x0, waiting for transfers between devices: 29.8 us -> none  [on_device(): lax.all_to_all(stacked, 'tm', split_axis=1, concat_axis=1, tiled=True)]
  transfers between devices with their start and end apart: 6 -> 5, of which waited for: 5 -> 4; matrix products, arithmetic and copies ran while one was open for 1% -> 3% of each run, Pallas kernels for 0% -> 30%
where the time goes in v1:
time: 217 us; the launch traced here: 219 us
  Pallas kernels  165 us (76%)
  waiting for transfers between devices  26 us (12%)
  starting transfers between devices  10.9 us (5%)
  other arithmetic  8.96 us (4%)
  matrix products  4.12 us (2%)
  local copies, waits for them, and re-layouts  2.9 us (1%)
    pallas_call x1, Pallas kernels, scatter(): pl.pallas_call(functools.partial(scatter_kernel, shards, groups), out_sha...  54 us
    pallas_call x1, Pallas kernels, attend(): pl.pallas_call(attend_kernel, grid_spec=pltpu.PrefetchScalarGridSpec(num_...  53.3 us
    pallas_call x1, Pallas kernels, reduce_all(): pl.pallas_call(functools.partial(reduce_kernel, shards, groups), out_shap...  46.5 us
    pallas_call x1, Pallas kernels, sort_rows(): pl.pallas_call(sort_kernel, grid=(steps,), out_shape=jax.ShapeDtypeStruct...  11.5 us
    ppermute x1, waiting for transfers between devices, on_device(): left = lax.ppermute(own[trows:], 'tm', up)  9.83 us
    ppermute x1, waiting for transfers between devices, on_device(): lax.ppermute(lax.dynamic_slice_in_dim(od, (1 - half) * rows, rows, axis=0...  5.93 us
    ppermute x1, waiting for transfers between devices, on_device(): right = lax.ppermute(own[:trows], 'tm', down)  5.17 us
    ppermute x1, waiting for transfers between devices, on_device(): lax.ppermute(lax.dynamic_slice_in_dim(grad, (1 - half) * 128, 128, axis=1...  5.07 us
  transfers between devices with their start and end apart: 5, of which 4 were waited for; matrix products, arithmetic and copies ran while one was open for 3% of the time, Pallas kernels for 30%

profile of v1, /device:TPU:0, one launch (start us, length us, event | category | flops | bytes accessed | tf_op | source)
XLA Modules:
  0.0 219.0 jit_solution(14801409585125303574)
XLA Ops:
  1.3 3.1 %collective-permute-start = (s32[2,16]{1,0:T(2,128)S(1)}, s32[2,16]{1,0:T(2,128)S(1)}, u32[]{:S(2)}, u32[]{:S(2)}) collective-permute-start(s32[2,16]{1,0:T(2,128)S(1)} %pad_add_fusion), channel_id=1, source_target_pairs={{0,4},{4,0},{8,12},{12,8},{16,20},{20,16},{24,28},{28,24},{32,36},... | collective-permute-start | bytes 392 | tf_op jit(solution)/shard_map/ppermute | solution.py:513
  4.4 1.3 fusion.4.idx_ref
  5.8 54.0 %scatter.1 = (bf16[2,32,64,256]{3,2,1,0:T(8,128)(2,1)}, bf16[512,1024]{1,0:T(8,128)(2,1)}, bf16[4,256,256]{2,1,0:T(8,128)(2,1)}, bf16[2,512,128]{2,1,0:T(8,128)(2,1)}) custom-call(bf16[32,64,256]{2,1,0:T(8,128)(2,1)} %bitcast.27, bf16[32,64,256]{2,1,0:T(8,128)(2,1)} %bitcast.28, bf16[512,256]{1,0:T(8,128)(2,1)} %sq.1, bf16[512,256]{1,0:T(8,128)(2,1)} %cot.1, ...), custom_call_target="tpu_custom_call" | custom-call | tf_op jit(solution)/shard_map/scatter/pallas_call | solution.py:150
  59.8 11.5 %sort_rows.1.own = bf16[4096,256]{1,0:T(8,128)(2,1)} custom-call(s32[32,128]{1,0:T(8,128)} %fusion.4.idx_ref, bf16[4096,256]{1,0:T(8,128)(2,1)} %bitcast.33), custom_call_target="tpu_custom_call" | custom-call | flops 4294967296 | bytes 4194304 | tf_op jit(solution)/shard_map/sort_rows/pallas_call | solution.py:194
  71.3 1.8 fusion.9
  73.2 3.6 %collective-permute-start.1 = (bf16[2048,256]{1,0:T(8,128)(2,1)S(1)}, bf16[2048,256]{1,0:T(8,128)(2,1)}, u32[]{:S(2)}, u32[]{:S(2)}) collective-permute-start(bf16[2048,256]{1,0:T(8,128)(2,1)S(1)} %get-tuple-element.16), channel_id=1, source_target_pairs={{0,8},{4,12},{8,16},{12,20},{16,24},{20,28},{24,32},{28,36},{32,40... | collective-permute-start | bytes 3145736 | tf_op jit(solution)/shard_map/ppermute | solution.py:497
  76.7 1.3 collective-permute-start.2
  78.6 1.0 collective-permute-start.3
  80.2 5.1 %collective-permute-done.3 = bf16[512,128]{1,0:T(8,128)(2,1)} collective-permute-done((bf16[512,128]{1,0:T(8,128)(2,1)S(1)}, bf16[512,128]{1,0:T(8,128)(2,1)}, u32[]{:S(2)}, u32[]{:S(2)}) %collective-permute-start.3) | collective-permute-done | bytes 131104 | tf_op jit(solution)/shard_map/ppermute | solution.py:504
  85.2 1.0 broadcast_select_fusion.3
  86.2 0.7 pad_maximum_fusion.g_ref
  86.9 9.8 %collective-permute-done.1.left = bf16[2048,256]{1,0:T(8,128)(2,1)} collective-permute-done((bf16[2048,256]{1,0:T(8,128)(2,1)S(1)}, bf16[2048,256]{1,0:T(8,128)(2,1)}, u32[]{:S(2)}, u32[]{:S(2)}) %collective-permute-start.1) | collective-permute-done | bytes 1048608 | tf_op jit(solution)/shard_map/ppermute | solution.py:497
  96.7 5.2 %collective-permute-done.2.right = bf16[2048,256]{1,0:T(8,128)(2,1)} collective-permute-done((bf16[2048,256]{1,0:T(8,128)(2,1)S(1)}, bf16[2048,256]{1,0:T(8,128)(2,1)}, u32[]{:S(2)}, u32[]{:S(2)}) %collective-permute-start.2) | collective-permute-done | bytes 1048608 | tf_op jit(solution)/shard_map/ppermute | solution.py:498
  101.9 53.3 %attend.1 = bf16[1024,256]{1,0:T(8,128)(2,1)} custom-call(s32[32]{0:T(128)} %get-tuple-element.28.lo_ref, s32[32]{0:T(128)} %get-tuple-element.27.hi_ref, bf16[2048,256]{1,0:T(8,128)(2,1)} %collective-permute-done.1.left, bf16[4096,256]{1,0:T(8,128)(2,1)} %sort_rows.1.own, bf16[2048,256]{1,0:T(8,128)(2,1)} %collective-permute-done.2.right, ...), custom_call_target="tpu_custom_call" | custom-call | flops 8589934592 | bytes 6291456 | tf_op jit(solution)/shard_map/attend/pallas_call | solution.py:324
  155.2 1.0 constant_dynamic-slice_fusion
  156.1 2.0 collective-permute-start.4
  158.2 5.9 %collective-permute-done.4 = bf16[512,256]{1,0:T(8,128)(2,1)S(1)} collective-permute-done((bf16[512,256]{1,0:T(8,128)(2,1)S(1)}, bf16[512,256]{1,0:T(8,128)(2,1)S(1)}, u32[]{:S(2)}, u32[]{:S(2)}) %collective-permute-start.4) | collective-permute-done | bytes 262176 | tf_op jit(solution)/shard_map/ppermute | solution.py:527
  164.1 1.0 broadcast_select_fusion.1
  165.3 1.3 fusion.wg
  166.5 0.7 pad_maximum_fusion.1.o_ref
  167.3 46.5 %reduce_all.1 = (bf16[32,8,1024]{2,1,0:T(8,128)(2,1)}, bf16[512,1024]{1,0:T(8,128)(2,1)}) custom-call(bf16[32,8,1024]{2,1,0:T(8,128)(2,1)} %fusion.wg, bf16[512,256]{1,0:T(8,128)(2,1)} %pad_maximum_fusion.1.o_ref), custom_call_target="tpu_custom_call" | custom-call | tf_op jit(solution)/shard_map/reduce_all/pallas_call | solution.py:443
  213.8 2.1 bitcast_convert_fusion
  215.9 2.4 %convolution_convert_fusion.1 = bf16[512,256]{1,0:T(8,128)(2,1)} fusion(bf16[512,1024]{1,0:T(8,128)(2,1)} %get-tuple-element.12, bf16[1024,256]{1,0:T(8,128)(2,1)S(1)} %bitcast.34), kind=kOutput, calls=%fused_computation.2 | convolution fusion | flops 268566528 | bytes 1835008 | tf_op jit(solution)/shard_map/dot_general | solution.py:541
  218.3 0.7 pad_maximum_fusion.2
  (18 shorter events, 1.9 us)
Async XLA Ops:
  1.3 78.2 %collective-permute-start = (s32[2,16]{1,0:T(2,128)S(1)}, s32[2,16]{1,0:T(2,128)S(1)}, u32[]{:S(2)}, u32[]{:S(2)}) collective-permute-start(s32[2,16]{1,0:T(2,128)S(1)} %pad_add_fusion), channel_id=1, source_target_pairs={{0,4},{4,0},{8,12},{12,8},{16,20},{20,16},{24,28},{28,24},{32,36},... | collective-permute-start | bytes 392 | tf_op jit(solution)/shard_map/ppermute | solution.py:513
  71.3 6.7 %copy-start = (bf16[512,1024]{1,0:T(8,128)(2,1)S(1)}, bf16[512,1024]{1,0:T(8,128)(2,1)}, u32[]{:S(2)}) copy-start(bf16[512,1024]{1,0:T(8,128)(2,1)} %get-tuple-element.11) | copy-start | bytes 3145732
  71.3 6.7 %copy-start.1 = (bf16[256,1024]{1,0:T(8,128)(2,1)S(1)}, bf16[256,1024]{1,0:T(8,128)(2,1)}, u32[]{:S(2)}) copy-start(bf16[256,1024]{1,0:T(8,128)(2,1)} %ow.1) | copy-start | bytes 1572868
  73.1 6.4 %copy-start.2 = (s32[16]{0:T(128)S(1)}, s32[16]{0:T(128)}, u32[]{:S(2)}) copy-start(s32[16]{0:T(128)} %param.13) | copy-start | bytes 196
  73.2 6.4 %copy-start.3 = (s32[16]{0:T(128)S(1)}, s32[16]{0:T(128)}, u32[]{:S(2)}) copy-start(s32[16]{0:T(128)} %param.12) | copy-start | bytes 196
  73.2 23.6 %collective-permute-start.1 = (bf16[2048,256]{1,0:T(8,128)(2,1)S(1)}, bf16[2048,256]{1,0:T(8,128)(2,1)}, u32[]{:S(2)}, u32[]{:S(2)}) collective-permute-start(bf16[2048,256]{1,0:T(8,128)(2,1)S(1)} %get-tuple-element.16), channel_id=1, source_target_pairs={{0,8},{4,12},{8,16},{12,20},{16,24},{20,28},{24,32},{28,36},{32,40... | collective-permute-start | bytes 3145736 | tf_op jit(solution)/shard_map/ppermute | solution.py:497
  76.7 25.2 %collective-permute-start.2 = (bf16[2048,256]{1,0:T(8,128)(2,1)S(1)}, bf16[2048,256]{1,0:T(8,128)(2,1)}, u32[]{:S(2)}, u32[]{:S(2)}) collective-permute-start(bf16[2048,256]{1,0:T(8,128)(2,1)S(1)} %get-tuple-element.15), channel_id=1, source_target_pairs={{8,0},{12,4},{16,8},{20,12},{24,16},{28,20},{32,24},{36,28},{40,32... | collective-permute-start | bytes 3145736 | tf_op jit(solution)/shard_map/ppermute | solution.py:498
  78.6 6.7 %collective-permute-start.3 = (bf16[512,128]{1,0:T(8,128)(2,1)S(1)}, bf16[512,128]{1,0:T(8,128)(2,1)}, u32[]{:S(2)}, u32[]{:S(2)}) collective-permute-start(bf16[512,128]{1,0:T(8,128)(2,1)S(1)} %constant_dynamic-slice_fusion.1), channel_id=1, source_target_pairs={{0,4},{4,0},{8,12},{12,8},{16,20},{20,16},{24,28},{28,24},{32,36},... | collective-permute-start | bytes 393224 | tf_op jit(solution)/shard_map/ppermute | solution.py:504
  156.1 8.0 %collective-permute-start.4 = (bf16[512,256]{1,0:T(8,128)(2,1)S(1)}, bf16[512,256]{1,0:T(8,128)(2,1)S(1)}, u32[]{:S(2)}, u32[]{:S(2)}) collective-permute-start(bf16[512,256]{1,0:T(8,128)(2,1)S(1)} %constant_dynamic-slice_fusion), channel_id=1, source_target_pairs={{0,4},{4,0},{8,12},{12,8},{16,20},{20,16},{24,28},{28,24},{32,36},... | collective-permute-start | bytes 786440 | tf_op jit(solution)/shard_map/ppermute | solution.py:527
  165.2 50.7 %copy-start.4 = (bf16[4,256,256]{2,1,0:T(8,128)(2,1)S(1)}, bf16[4,256,256]{2,1,0:T(8,128)(2,1)}, u32[]{:S(2)}) copy-start(bf16[4,256,256]{2,1,0:T(8,128)(2,1)} %get-tuple-element.13) | copy-start | bytes 1572868

commit v2 on v0

v2 whole, which is shorter than its diff:
```python
import functools
import math

import jax
import jax.numpy as jnp
from jax import lax
from jax.experimental import pallas as pl
from jax.experimental.pallas import tpu as pltpu
from jax.sharding import PartitionSpec as P

HDIM = 64
SBLK = 32
TBLK = 128
F = 128
CH = 1024
GROUP = 1024
ANY = pl.BlockSpec(memory_space=pl.ANY)
MESH = pl.DeviceIdType.MESH


def greet(shards, bits):
    me = lax.axis_index("tm")
    c = lax.axis_index("clip")
    barrier = pltpu.get_barrier_semaphore()

    def tell(d, carry):
        pl.semaphore_signal(
            barrier, inc=1, device_id={"tm": lax.rem(me + d, shards)}, device_id_type=MESH
        )
        return carry

    lax.fori_loop(1, shards, tell, 0)
    for bit in bits:
        pl.semaphore_signal(
            barrier, inc=1, device_id={"clip": flip(c, bit)}, device_id_type=MESH
        )
    pl.semaphore_wait(barrier, shards - 1 + len(bits))


def flip(c, bit):
    if bit == 3:
        return 3 - c
    return c + bit - 2 * bit * lax.rem(lax.div(c, bit), 2)


def send(src, dst, sems, **where):
    return pltpu.make_async_remote_copy(
        src_ref=src, dst_ref=dst, send_sem=sems[0], recv_sem=sems[1],
        device_id=where, device_id_type=MESH,
    )


def exchange_kernel(
    shards, tk, tv, sq, cot, ow, bands,
    kv, left, right, cotf, wcols, qp, gp, bp,
    cotv, wv, gv, ks, kr, vs, vr, ls, lr, rs, rr, cs, ws, wr, ms, os_,
):
    me = lax.axis_index("tm")
    c = lax.axis_index("clip")
    half = lax.rem(me, 2)
    mate = flip(me, 1)
    pair = lax.div(me, 2)
    groups, rows, wide = cotv.shape
    near, far = flip(c, 1), flip(c, 2)
    across = flip(far, 1)
    prev = lax.rem(me + shards - 2, shards)
    after = lax.rem(me + 2, shards)
    greet(shards, (1, 2, 3))

    def key_copies(target, slot, src):
        p = lax.div(target, 2)
        col = pl.multiple_of(lax.rem(target, 2) * 128, 128)
        return (
            send(
                tk.at[pl.ds(2 * p, 2), :, pl.ds(col, 128)],
                kv.at[:, me, :, pl.ds(0, 128)], (ks.at[slot], kr.at[src]), tm=target,
            ),
            send(
                tv.at[pl.ds(2 * p, 2), :, pl.ds(col, 128)],
                kv.at[:, me, :, pl.ds(128, 128)], (vs.at[slot], vr.at[src]), tm=target,
            ),
        )

    def halo_copies(s):
        return (
            send(kv.at[0, s], right.at[s], (rs.at[s], rr.at[s]), tm=prev),
            send(kv.at[1, s], left.at[s], (ls.at[s], lr.at[s]), tm=after),
        )

    def w_copy(d, src):
        target = lax.rem(c + d, groups)
        theirs = pl.multiple_of(target * wide, 128)
        return send(
            ow.at[:, pl.ds(theirs, wide)], wcols.at[c], (ws.at[d], wr.at[src]), clip=target
        )

    own = pl.multiple_of(half * 128, 128)
    other = pl.multiple_of((1 - half) * 128, 128)
    mine = pl.multiple_of(c * wide, 128)
    cot_far = send(cot, cotv.at[c], (cs.at[0], cs.at[1]), clip=far)
    cot_near = send(cot, cotv.at[c], (cs.at[2], cs.at[3]), clip=near)
    cot_relay = send(cotv.at[far], cotv.at[far], (cs.at[4], cs.at[5]), clip=near)
    q_copy = send(sq.at[:, pl.ds(other, 128)], qp.at[half], (ms.at[0], ms.at[1]), tm=mate)
    b_copy = send(bands, bp.at[half], (ms.at[2], ms.at[3]), tm=mate)
    g_copy = send(gv.at[1 - half], gp.at[half], (ms.at[4], ms.at[5]), tm=mate)

    cot_far.start()
    cot_near.start()

    def start(d, carry):
        for copy in key_copies(lax.rem(me + d, shards), d, me):
            copy.start()
        return carry

    lax.fori_loop(1, shards, start, 0)
    q_copy.start()
    b_copy.start()
    for d in range(1, groups):
        w_copy(d, c).start()
    mine_kv = (
        pltpu.make_async_copy(
            tk.at[pl.ds(2 * pair, 2), :, pl.ds(own, 128)], kv.at[:, me, :, pl.ds(0, 128)], os_.at[0]
        ),
        pltpu.make_async_copy(
            tv.at[pl.ds(2 * pair, 2), :, pl.ds(own, 128)], kv.at[:, me, :, pl.ds(128, 128)], os_.at[1]
        ),
    )
    mine_cot = (
        pltpu.make_async_copy(cot, cotv.at[c], os_.at[2]),
        pltpu.make_async_copy(ow, wv, os_.at[3]),
    )
    mine_rest = (
        pltpu.make_async_copy(ow.at[:, pl.ds(mine, wide)], wcols.at[c], os_.at[4]),
        pltpu.make_async_copy(sq.at[:, pl.ds(own, 128)], qp.at[half], os_.at[5]),
        pltpu.make_async_copy(bands, bp.at[half], os_.at[6]),
    )
    for copy in mine_cot + mine_kv + mine_rest:
        copy.start()
    for copy in mine_cot + mine_kv:
        copy.wait()
    for copy in halo_copies(me):
        copy.start()
    cot_far.wait_recv()
    cot_relay.start()
    cot_near.wait_recv()
    cot_relay.wait_recv()
    nt = (((1,), (1,)), ((), ()))
    grad = jnp.zeros((rows, wide), jnp.float32)
    for j in range(groups):
        grad += lax.dot_general(
            cotv[j], wv[:, j * wide : (j + 1) * wide], nt, preferred_element_type=jnp.float32
        )
    gv[0] = grad[:, 0:128].astype(jnp.bfloat16)
    gv[1] = grad[:, 128:256].astype(jnp.bfloat16)
    put_cot = pltpu.make_async_copy(cotv, cotf, os_.at[7])
    put_cot.start()

    def forward(d, carry):
        s = lax.rem(me + shards - d, shards)
        for copy in key_copies(lax.rem(me + d, shards), d, s):
            copy.wait_recv()
        for copy in halo_copies(s):
            copy.start()
        return carry

    lax.fori_loop(1, 3, forward, 0)
    g_copy.start()
    put_g = pltpu.make_async_copy(gv.at[half], gp.at[half], os_.at[8])
    put_g.start()
    lax.fori_loop(3, shards, forward, 0)

    def finish(d, carry):
        s = lax.rem(me + shards - d, shards)
        for copy in key_copies(lax.rem(me + d, shards), d, s):
            copy.wait_send()
        return carry

    lax.fori_loop(1, shards, finish, 0)
    for copy in mine_rest:
        copy.wait()
    put_cot.wait()
    put_g.wait()
    cot_far.wait_send()
    cot_near.wait_send()
    cot_relay.wait_send()
    q_copy.wait()
    b_copy.wait()
    g_copy.wait()
    for d in range(1, groups):
        w_copy(d, lax.rem(c + groups - d, groups)).wait()

    def arrive(s, carry):
        for copy in halo_copies(s):
            copy.wait()
        return carry

    lax.fori_loop(0, shards, arrive, 0)


def exchange(tk, tv, sq, cot, ow, bands, shards, groups):
    bf = jnp.bfloat16
    rows, wide = sq.shape
    piece = tk.shape[1]
    dma = pltpu.SemaphoreType.DMA
    halo = jax.ShapeDtypeStruct((shards, piece, 256), bf)
    return pl.pallas_call(
        functools.partial(exchange_kernel, shards),
        out_shape=(
            jax.ShapeDtypeStruct((2, shards, piece, 256), bf),
            halo,
            halo,
            jax.ShapeDtypeStruct((groups, rows, wide), bf),
            jax.ShapeDtypeStruct((groups, wide, wide), bf),
            jax.ShapeDtypeStruct((2, rows, 128), bf),
            jax.ShapeDtypeStruct((2, rows, 128), bf),
            jax.ShapeDtypeStruct((2,) + bands.shape, jnp.int32),
        ),
        in_specs=[ANY] * 6,
        out_specs=(ANY,) * 8,
        scratch_shapes=[
            pltpu.VMEM((groups, rows, wide), bf),
            pltpu.VMEM((wide, groups * wide), bf),
            pltpu.VMEM((2, rows, 128), bf),
        ]
        + [dma((shards,))] * 8
        + [dma((6,)), dma((groups,)), dma((groups,)), dma((6,)), dma((9,))],
        compiler_params=pltpu.CompilerParams(collective_id=0, has_side_effects=True),
        name="exchange",
    )(tk, tv, sq, cot, ow, bands)


def attend_kernel(
    tiles, shards, lo_ref, hi_ref, left, own, right, order, q_ref, g_ref, gp_ref, o_ref, dq_ref,
    arr, idx, hot, kv, kvt, s_scr, d_scr, p_scr, qb, gb, top_scr, stat_scr, sem,
):
    t = pl.program_id(0)
    f32 = jnp.float32
    bf = jnp.bfloat16
    L = 2 * F
    nb = F // SBLK
    per = CH // TBLK
    pad = kv.shape[0] - CH
    side = arr.shape[1]
    piece = side // shards
    irows = side // 128

    @pl.when(t == 0)
    def _():
        pair = lax.div(lax.axis_index("tm"), 2)
        copies = [
            pltpu.make_async_copy(left, arr.at[0], sem.at[0]),
            pltpu.make_async_copy(own.at[0], arr.at[1], sem.at[1]),
            pltpu.make_async_copy(own.at[1], arr.at[2], sem.at[2]),
            pltpu.make_async_copy(right, arr.at[3], sem.at[3]),
        ]
        for e in range(4):
            shard = lax.rem(2 * pair + shards - 1 + e, shards)
            at = pl.multiple_of(shard * irows, irows)
            copies.append(
                pltpu.make_async_copy(
                    order.at[pl.ds(at, irows)], idx.at[pl.ds(e * irows, irows)], sem.at[4 + e]
                )
            )
        for copy in copies:
            copy.start()
        kv[pad : pad + CH, :] = jnp.zeros((CH, 256), bf)
        kvt[:, pad : pad + CH] = jnp.zeros((256, CH), bf)
        for copy in copies:
            copy.wait()
        lane = lax.broadcasted_iota(jnp.int32, (128, 128), 1)

        def sort(j, carry):
            for r in range(GROUP // 128):
                row = idx[pl.ds(j * (GROUP // 128) + r, 1), :]
                col = jnp.broadcast_to(row, (128, 128)).T
                at = lax.div(col, side) * piece + lax.rem(col, piece)
                base = jnp.where(lax.rem(at, 128) == lane, lax.div(at, 128), -1)
                base = base.astype(f32).astype(bf)
                for k in range(side // 128):
                    hot[r * 128 : (r + 1) * 128, k * 128 : (k + 1) * 128] = jnp.where(
                        base == bf(k), bf(1), bf(0)
                    )
            e = lax.div(j * GROUP, side)
            rows = jnp.dot(hot[...], arr[e], preferred_element_type=f32)
            at = pl.multiple_of(j * GROUP, GROUP)
            kv[pl.ds(at, GROUP), :] = rows.astype(bf)
            kvt[:, pl.ds(at, GROUP)] = rows.T.astype(bf)
            return carry

        lax.fori_loop(0, pad // GROUP, sort, 0)

    def bounds(tile):
        los = [lo_ref[nb * tile + r] for r in range(nb)]
        his = [hi_ref[nb * tile + r] for r in range(nb)]
        low = functools.reduce(jnp.minimum, los)
        high = functools.reduce(jnp.maximum, his)
        return los, his, low, (high - low) // per + 1

    n = functools.reduce(jnp.maximum, [bounds(x)[3] for x in range(tiles)])
    lane = lax.broadcasted_iota(jnp.int32, (F, 128), 1)
    zero = jnp.zeros((F, 128), bf)
    nt = (((1,), (1,)), ((), ()))
    slot = lax.rem(t, 2)

    def start_at(first, k):
        return pl.multiple_of(jnp.minimum(first * TBLK + k * CH, pad), TBLK)

    def split_heads(x):
        return jnp.where(lane < HDIM, x, zero), jnp.where(lane < HDIM, zero, x)

    def join_heads(x):
        x = x.T
        return jnp.where(lane < HDIM, x[0:F], x[F:L])

    def step(do1, do2, do3):
        if do1:
            los, his, first1, _ = bounds(t)
            qb[0:F, :], qb[F:L, :] = split_heads(q_ref[...] * bf(1.0 / math.sqrt(HDIM)))
            gb[0:F, :], gb[F:L, :] = split_heads(g_ref[...])
            frame = lax.rem(lax.broadcasted_iota(jnp.int32, (8, L), 1), F) // SBLK
            lov = jnp.full((8, L), los[0], jnp.int32)
            hiv = jnp.full((8, L), his[0], jnp.int32)
            for r in range(1, nb):
                lov = jnp.where(frame == r, los[r], lov)
                hiv = jnp.where(frame == r, his[r], hiv)
        if do2:
            first2 = bounds(t - 1)[2]
            top2 = top_scr[...]
        if do3:
            first3 = bounds(t - 2)[2]
            delta = stat_scr[0]

        def body(k, carry):
            top, total, o, dq = carry
            at = pl.multiple_of(k * CH, CH)
            if do3:
                base = start_at(first3, k)
                e = p_scr[pl.ds(at, CH), :].astype(f32).reshape(CH // 8, 8, L)
                d = d_scr[slot, pl.ds(at, CH), :].reshape(CH // 8, 8, L)
                ds = (e * (d - delta[None])).reshape(CH, L).astype(bf)
                dq = dq + jnp.dot(kvt[0:128, pl.ds(base, CH)], ds, preferred_element_type=f32)
            if do2:
                base = start_at(first2, k)
                s = s_scr[pl.ds(at, CH), :].reshape(CH // 8, 8, L)
                e = jnp.exp(s - top2[None]).reshape(CH, L).astype(bf)
                p_scr[pl.ds(at, CH), :] = e
                total = total + jnp.sum(e.astype(f32).reshape(CH // 8, 8, L), axis=0)
                o = o + jnp.dot(kvt[128:256, pl.ds(base, CH)], e, preferred_element_type=f32)
            if do1:
                base = start_at(first1, k)
                s = lax.dot_general(
                    kv[pl.ds(base, CH), 0:128], qb[...], nt, preferred_element_type=f32
                )
                d_scr[slot, pl.ds(at, CH), :] = lax.dot_general(
                    kv[pl.ds(base, CH), 128:256], gb[...], nt, preferred_element_type=f32
                )
                for c in range(per):
                    block = first1 + k * per + c
                    ok = (block >= lov) & (block <= hiv)
                    bias = jnp.where(ok, 0.0, -jnp.inf).astype(f32)
                    part = s[c * 128 : (c + 1) * 128].reshape(16, 8, L) + bias[None]
                    s_scr[pl.ds(at + c * 128, 128), :] = part.reshape(128, L)
                    top = jnp.maximum(top, jnp.max(part, axis=0))
            return top, total, o, dq

        flat = jnp.zeros((8, L), f32)
        acc = jnp.zeros((128, L), f32)
        top, total, o, dq = lax.fori_loop(
            0, n, body, (jnp.full((8, L), -jnp.inf, f32), flat, acc, acc)
        )
        if do3:
            scale = stat_scr[1][0:1] * (1.0 / math.sqrt(HDIM))
            dq_ref[...] = join_heads(dq * scale).astype(bf)
        if do2:
            inv = 1.0 / jnp.sum(total, axis=0, keepdims=True)
            o = o * inv
            o_ref[...] = join_heads(o).astype(bf)
            grad = jnp.concatenate(split_heads(gp_ref[...]), axis=0).astype(f32).T
            stat_scr[0] = jnp.broadcast_to(jnp.sum(o * grad, axis=0, keepdims=True), (8, L))
            stat_scr[1] = jnp.broadcast_to(inv, (8, L))
        if do1:
            top_scr[...] = jnp.broadcast_to(jnp.max(top, axis=0, keepdims=True), (8, L))

    pl.when(t == 0)(lambda: step(True, False, False))
    pl.when(t == 1)(lambda: step(True, True, False))
    pl.when((t >= 2) & (t < tiles))(lambda: step(True, True, True))
    pl.when(t == tiles)(lambda: step(False, True, True))
    pl.when(t == tiles + 1)(lambda: step(False, False, True))


def attend(lo, hi, left, own, right, order, q, g, shards):
    frames = q.shape[0]
    side = left.shape[0]
    window = 4 * side
    reach = side // TBLK
    bf = jnp.bfloat16
    f32 = jnp.float32
    L = 2 * F
    tiles = frames // F
    keys = ((2 * reach + F // SBLK - 1) // (CH // TBLK) + 1) * CH
    now = lambda i, lo, hi: (jnp.minimum(i, tiles - 1), 0)
    one = lambda i, lo, hi: (jnp.clip(i - 1, 0, tiles - 1), 0)
    two = lambda i, lo, hi: (jnp.clip(i - 2, 0, tiles - 1), 0)
    return pl.pallas_call(
        functools.partial(attend_kernel, tiles, shards),
        grid_spec=pltpu.PrefetchScalarGridSpec(
            num_scalar_prefetch=2,
            grid=(tiles + 2,),
            in_specs=[ANY] * 4
            + [pl.BlockSpec((F, 128), now), pl.BlockSpec((F, 128), now), pl.BlockSpec((F, 128), one)],
            out_specs=(pl.BlockSpec((F, 128), one), pl.BlockSpec((F, 128), two)),
            scratch_shapes=[
                pltpu.VMEM((4, side, 256), bf),
                pltpu.VMEM((window // 128, 128), jnp.int32),
                pltpu.VMEM((GROUP, side), bf),
                pltpu.VMEM((window + CH, 256), bf),
                pltpu.VMEM((256, window + CH), bf),
                pltpu.VMEM((keys, L), f32),
                pltpu.VMEM((2, keys, L), f32),
                pltpu.VMEM((keys, L), bf),
                pltpu.VMEM((L, 128), bf),
                pltpu.VMEM((L, 128), bf),
                pltpu.VMEM((8, L), f32),
                pltpu.VMEM((2, 8, L), f32),
                pltpu.SemaphoreType.DMA((8,)),
            ],
        ),
        out_shape=(jax.ShapeDtypeStruct((frames, 128), bf),) * 2,
        name="attend",
    )(lo, hi, left, own, right, order, q, g, g)


def finish_kernel(
    shards, o_ref, dq_ref, cot, wcols, joined, dq, wsum,
    og, wg, got, red, ss, sr, gs, gr, ms, cs, ls,
):
    me = lax.axis_index("tm")
    c = lax.axis_index("clip")
    half = lax.rem(me, 2)
    mate = flip(me, 1)
    near, far = flip(c, 1), flip(c, 2)
    groups, rows, wide = og.shape
    bf = jnp.bfloat16
    f32 = jnp.float32
    part_rows, part_cols = red.shape
    greet(shards, (1, 2))

    own = pl.multiple_of(half * 128, 128)
    my_rows = pl.multiple_of(half * rows, 128)
    mate_rows = pl.multiple_of((1 - half) * rows, 128)
    o_mate = send(
        o_ref.at[pl.ds(mate_rows, rows)], og.at[c, :, pl.ds(own, 128)], (ms.at[0], ms.at[1]), tm=mate
    )
    dq_mate = send(
        dq_ref.at[pl.ds(mate_rows, rows)], dq.at[:, pl.ds(own, 128)], (ms.at[2], ms.at[3]), tm=mate
    )
    o_own = pltpu.make_async_copy(
        o_ref.at[pl.ds(my_rows, rows)], og.at[c, :, pl.ds(own, 128)], ls.at[0]
    )
    dq_own = pltpu.make_async_copy(
        dq_ref.at[pl.ds(my_rows, rows)], dq.at[:, pl.ds(own, 128)], ls.at[1]
    )
    o_far = send(og.at[c], og.at[c], (cs.at[0], cs.at[1]), clip=far)
    o_near = send(og.at[c], og.at[c], (cs.at[2], cs.at[3]), clip=near)
    o_relay = send(og.at[far], og.at[far], (cs.at[4], cs.at[5]), clip=near)

    def part_copy(d, src):
        target = lax.rem(me + d, shards)
        return send(
            wg.at[lax.div(target, 2), lax.rem(target, 2)], got.at[me],
            (ss.at[d], sr.at[src]), tm=target,
        )

    def place():
        at = pl.multiple_of(lax.div(me, 2) * part_rows, part_rows)
        col = pl.multiple_of(half * part_cols, 128)
        return wsum.at[pl.ds(at, part_rows), pl.ds(col, part_cols)]

    def sum_copy(d, src):
        return send(red, place(), (gs.at[d], gr.at[src]), tm=lax.rem(me + d, shards))

    o_mate.start()
    o_own.start()
    dq_mate.start()
    dq_own.start()
    o_own.wait()
    o_mate.wait()
    tn = (((0,), (0,)), ((), ()))
    block = og[c]
    for j in range(groups):
        part = lax.dot_general(block, cot[j], tn, preferred_element_type=f32).astype(bf)
        lanes = (j * wide) % part_cols
        wg[:, (j * wide) // part_cols, :, lanes : lanes + wide] = part.reshape(
            shards // 2, part_rows, wide
        )
    o_far.start()
    o_near.start()

    def start(d, carry):
        part_copy(d, me).start()
        return carry

    lax.fori_loop(1, shards, start, 0)
    got[pl.ds(me, 1)] = wg[lax.div(me, 2), pl.ds(half, 1)]
    o_far.wait_recv()
    o_relay.start()

    def arrive(d, carry):
        part_copy(d, lax.rem(me + shards - d, shards)).wait_recv()
        return carry

    lax.fori_loop(1, shards, arrive, 0)

    def add(s, acc):
        return acc + got[s].astype(f32)

    red[...] = lax.fori_loop(0, shards, add, jnp.zeros(red.shape, f32)).astype(bf)
    o_near.wait_recv()
    o_relay.wait_recv()

    def start_sum(d, carry):
        sum_copy(d, me).start()
        return carry

    lax.fori_loop(1, shards, start_sum, 0)
    put = pltpu.make_async_copy(red, place(), ls.at[2])
    put.start()
    total = jnp.zeros((rows, wide), f32)
    for j in range(groups):
        total += jnp.dot(og[j], wcols[j], preferred_element_type=f32)
    joined[...] = total.astype(bf)

    def end(d, carry):
        part_copy(d, lax.rem(me + shards - d, shards)).wait_send()
        sum_copy(d, lax.rem(me + shards - d, shards)).wait()
        return carry

    lax.fori_loop(1, shards, end, 0)
    put.wait()
    o_far.wait_send()
    o_near.wait_send()
    o_relay.wait_send()
    dq_mate.wait()
    dq_own.wait()


def finish(o, dq, cot, wcols, shards):
    bf = jnp.bfloat16
    dma = pltpu.SemaphoreType.DMA
    groups, rows, wide = cot.shape
    cols = groups * wide
    pr, pc = wide // (shards // 2), cols // 2
    vmem = pl.BlockSpec(memory_space=pltpu.VMEM)
    return pl.pallas_call(
        functools.partial(finish_kernel, shards),
        out_shape=(
            jax.ShapeDtypeStruct((rows, wide), bf),
            jax.ShapeDtypeStruct((rows, wide), bf),
            jax.ShapeDtypeStruct((wide, cols), bf),
        ),
        in_specs=[ANY, ANY, vmem, vmem],
        out_specs=(vmem, ANY, ANY),
        scratch_shapes=[
            pltpu.VMEM((groups, rows, wide), bf),
            pltpu.VMEM((shards // 2, 2, pr, pc), bf),
            pltpu.VMEM((shards, pr, pc), bf),
            pltpu.VMEM((pr, pc), bf),
            dma((shards,)), dma((shards,)), dma((shards,)), dma((shards,)),
            dma((4,)), dma((6,)), dma((3,)),
        ],
        compiler_params=pltpu.CompilerParams(collective_id=1, has_side_effects=True),
        name="finish",
    )(o, dq, cot, wcols)


def on_device(
    student_query,
    teacher_key,
    teacher_value,
    clip_order,
    band_start,
    band_end,
    output_weight,
    cotangent,
):
    shards = lax.axis_size("tm")
    groups = lax.axis_size("clip")
    pair = lax.axis_index("tm") // 2
    rows, wide = student_query.shape
    trows = teacher_key.shape[0]
    piece = trows // shards
    blocks = rows // SBLK

    bands = jnp.pad(jnp.stack([band_start, band_end]), ((0, 6), (0, 128 - blocks)))
    kv, left, right, cot_full, w_cols, q_pair, g_pair, b_pair = exchange(
        teacher_key.reshape(shards, piece, wide),
        teacher_value.reshape(shards, piece, wide),
        student_query, cotangent, output_weight, bands, shards, groups,
    )
    starts = b_pair[:, 0, :blocks].reshape(2 * blocks)
    ends = b_pair[:, 1, :blocks].reshape(2 * blocks)
    reach = trows // TBLK
    base = pair * 2 * blocks
    at = reach + jnp.arange(2 * blocks, dtype=jnp.int32)
    lo = jnp.maximum(at + starts, reach - base)
    hi = jnp.minimum(at + ends, shards * blocks - 1 + reach - base)

    o, dq = attend(
        lo, hi,
        left.reshape(trows, 256), kv.reshape(2, trows, 256), right.reshape(trows, 256),
        clip_order.reshape(-1, 128),
        q_pair.reshape(2 * rows, 128), g_pair.reshape(2 * rows, 128), shards,
    )
    joined, grad_query, wsum = finish(o, dq, cot_full, w_cols, shards)
    return (joined, grad_query, wsum.astype(jnp.float32))


def solution(mesh):
    return jax.shard_map(
        on_device,
        mesh=mesh,
        in_specs=(
            P("tm", "clip"),
            P("tm", "clip"),
            P("tm", "clip"),
            P(),
            P("tm"),
            P("tm"),
            P("clip", None),
            P("tm", "clip"),
        ),
        out_specs=(P("tm", "clip"), P("tm", "clip"), P("clip", None)),
        check_vma=False,
    )
```

time: 945 us -> 161 us (0.17)
  waiting for transfers between devices: 503 us -> 0 us
  other arithmetic: 228 us -> 3.4 us
  Pallas kernels: 0 us -> 155 us
  local copies, waits for them, and re-layouts: 93.4 us -> 3.93 us
  matrix products: 72.4 us -> 0 us
  starting transfers between devices: 19.7 us -> 0 us
  between operations: 13.9 us -> 0.68 us
  loops' own time: 11.7 us -> 0 us
    psum x1 -> x0, waiting for transfers between devices: 357 us -> none  [on_device(): weight_grad = lax.psum(local_weight_grad, 'tm')]
    pallas_call x0 -> x3, Pallas kernels: none -> 155 us  [the longest x1 61.9 us: exchange(): pl.pallas_call(functools.partial(exchange_kernel, shards), out_shape=(jax...]
    sub x8 -> x0, other arithmetic: 95.5 us -> none  [the longest x4 71.7 us: attend_item(): dscores = (probs * (dprobs - delta) * scaling).astype(jnp.bfloat16)]
    dot_general x19 -> x0, matrix products: 72.4 us -> none  [the longest x4 23 us: attend_item(): jnp.einsum('hqk,khd->qhd', weights, value_part, preferred_element_type=jn...]
    reduce_scatter x1 -> x0, waiting for transfers between devices: 65.7 us -> none  [on_device(): lax.psum_scatter(jnp.dot(attention, output_weight, preferred_element_type...]
    add x12 -> x0, other arithmetic: 44.7 us -> none  [the longest x4 22.4 us: attend_item(): band_high = global_block + band_end[local_block]]
    gather x25 -> x0, other arithmetic: 36.2 us -> none  [the longest x24 36.2 us: attend_item(): band_low = global_block + band_start[local_block]]
    all_to_all x1 -> x0, waiting for transfers between devices: 29.8 us -> none  [on_device(): lax.all_to_all(stacked, 'tm', split_axis=1, concat_axis=1, tiled=True)]
  transfers between devices with their start and end apart: 6 -> 0, of which waited for: 5 -> 0; matrix products, arithmetic and copies ran while one was open for 1% -> 0% of each run, Pallas kernels for 0% -> 0%
where the time goes in v2:
time: 161 us; the launch traced here: 163 us
  Pallas kernels  155 us (96%)
  local copies, waits for them, and re-layouts  3.93 us (2%)
  other arithmetic  3.4 us (2%)
    pallas_call x1, Pallas kernels, exchange(): pl.pallas_call(functools.partial(exchange_kernel, shards), out_shape=(jax...  61.9 us
    pallas_call x1, Pallas kernels, finish(): pl.pallas_call(functools.partial(finish_kernel, shards), out_shape=(jax.S...  50 us
    pallas_call x1, Pallas kernels, attend(): pl.pallas_call(functools.partial(attend_kernel, tiles, shards), grid_spec...  43.2 us

profile of v2, /device:TPU:0, one launch (start us, length us, event | category | flops | bytes accessed | tf_op | source)
XLA Modules:
  0.0 163.1 jit_solution(13109269784050408905)
XLA Ops:
  0.6 0.7 pad_add_fusion
  1.3 0.6 pad.4.bands
  1.9 61.9 %exchange.1 = (bf16[2,32,64,256]{3,2,1,0:T(8,128)(2,1)}, bf16[32,64,256]{2,1,0:T(8,128)(2,1)}, bf16[32,64,256]{2,1,0:T(8,128)(2,1)}, bf16[4,512,256]{2,1,0:T(8,1...) custom-call(bf16[32,64,256]{2,1,0:T(8,128)(2,1)} %bitcast.13, ...), custom_call_target="tpu_custom_call" | custom-call | tf_op jit(solution)/shard_map/exchange/pallas_call | solution.py:206
  63.9 0.8 slice_reduce_fusion
  64.7 0.1 reshape_squeeze.7
  64.7 0.1 reshape_squeeze.6
  64.8 0.5 add_minimum_fusion
  65.4 43.2 %attend.1 = (bf16[1024,128]{1,0:T(8,128)(2,1)}, bf16[1024,128]{1,0:T(8,128)(2,1)}) custom-call(s32[32]{0:T(128)} %get-tuple-element.32.lo_ref, s32[32]{0:T(128)} %get-tuple-element.31.hi_ref, bf16[2048,256]{1,0:T(8,128)(2,1)} %bitcast.15, bf16[2,2048,256]{2,1,0:T(8,128)(2,1)} %bitcast.10, bf16[2048,256]{1,0:T(8,128)(2,1)} %bitcast.16, s32[512,128]{1,0:T(8,128)} %bitcast.17, ...), custom_call_target="tpu_custom_call" | custom-call | tf_op jit(solution)/shard_map/attend/pallas_call | solution.py:404
  108.5 50.0 %finish.1 = (bf16[512,256]{1,0:T(8,128)(2,1)}, bf16[512,256]{1,0:T(8,128)(2,1)}, bf16[256,1024]{1,0:T(8,128)(2,1)}) custom-call(bf16[1024,128]{1,0:T(8,128)(2,1)} %get-tuple-element.22.o_ref, bf16[1024,128]{1,0:T(8,128)(2,1)} %get-tuple-element.23.dq_ref, bf16[4,512,256]{2,1,0:T(8,128)(2,1)} %get-tuple-element.24.cot, ...), custom_call_target="tpu_custom_call" | custom-call | tf_op jit(solution)/shard_map/finish/pallas_call | solution.py:554
  158.6 0.0 copy-start
  158.6 2.2 %convert_element_type.3 = f32[256,1024]{1,0:T(8,128)} convert(bf16[256,1024]{1,0:T(8,128)(2,1)} %get-tuple-element.28) | non-fusion elementwise | flops 262144 | bytes 1572864 | tf_op jit(solution)/shard_map/convert_element_type | solution.py:615
  160.8 1.7 %copy.13 = bf16[512,256]{1,0:T(8,128)(2,1)} copy(bf16[512,256]{1,0:T(8,128)(2,1)} %get-tuple-element.36) | data formatting | bytes 524288
  162.4 0.0 copy-done
  162.4 0.7 copy.14
Async XLA Ops:
  158.6 3.9 %copy-start = (bf16[512,256]{1,0:T(8,128)(2,1)S(1)}, bf16[512,256]{1,0:T(8,128)(2,1)}, u32[]{:S(2)}) copy-start(bf16[512,256]{1,0:T(8,128)(2,1)} %get-tuple-element.37) | copy-start | bytes 786436
